TPU v7x, 256 devices: a whole 4x4x8 slice. The times are simulated.
256 devices in a mesh: cluster: 8 (over z), sub: 32 (over x, y, core).
Axes of the slice: x: 4, y: 4, z: 8, core: 2. Of those that a mesh axis runs over, the one named last changes fastest.
Arguments:
- dual_ops: bfloat16 [8, 32, 2048, 2048], P('cluster', 'sub'), as said below
- corner_coupling: float32 [8, 32, 48, 2048], P('cluster', 'sub'), may hold values from -0.3 to 0.3
- coarse_inverse: float32 [32, 128, 128], P('sub'), as said below
- corner_map: int32 [8, 32, 48], P('cluster', 'sub'), may hold values from 0 to 127, as said below
- interface_tiles: int32 [8, 32, 4], P('cluster', 'sub'), may hold values from 1 to 4, as said below
- gap_terms: float32 [8, 32, 2048, 128], P('cluster', 'sub')
Outputs:
- multipliers: float32 [8, 32, 2048, 128], P('cluster', 'sub')
- residual: float32 [8, 32, 2048, 128], P('cluster', 'sub')
Inputs may be any that keep to these rules, and one draw needn't show every extreme that they name: interface_tiles[c, s, k] counts the tiles that subdomain (c, s) shares with the subdomain at sub distance -2, -1, +1, +2 for k = 0..3, wrapping around 32; the count for distance +d equals that neighbour's count for distance -d; in every c some subdomain has 4 for all four. `corner_map`: the 48 entries of one subdomain are distinct. `dual_ops`: each matrix is symmetric positive definite. `coarse_inverse`: each matrix is symmetric positive definite.
All inputs are finite; a program needn't handle non-finite values.
Results may differ from a plain program's by a relative error of at most 0.009.
Values sent between devices are 32-bit elements; how exact they have to be, the bound alone decides.
No kernel may reach another device: no remote copies, remote signals or barrier semaphores. Data moves between devices by JAX's collectives and lax.ppermute only.
A program may use at most 64 MiB of HBM per device.

v0:
```python
import jax
import jax.numpy as jnp
from jax import lax
from jax.sharding import PartitionSpec as P

TILE = 128
MAXT = 4
NCOARSE = 128
ITERS = 3


def passed_along(block, axis, distance):
    devices = range(lax.axis_size(axis))
    route = [((i - distance) % len(devices), i) for i in devices]
    return lax.ppermute(block, axis, route)


def extract_run(values_in, start_row, row_count):
    run_rows = MAXT * TILE
    run_block = lax.dynamic_slice_in_dim(values_in, start_row, run_rows, 0)
    keep_mask = jnp.arange(run_rows, dtype=jnp.int32)[:, None] < row_count
    return jnp.where(keep_mask, run_block, jnp.zeros_like(run_block))


def insert_run(run_block, start_row, dual_rows):
    padded = jnp.zeros((dual_rows + run_block.shape[0], run_block.shape[1]), run_block.dtype)
    return lax.dynamic_update_slice_in_dim(padded, run_block, start_row, 0)[:dual_rows]


def local(dual_ops, corner_coupling, coarse_inverse, corner_map, interface_tiles, gap_terms):
    highest = lax.Precision.HIGHEST
    operator = dual_ops[0, 0]
    coupling = corner_coupling[0, 0]
    inverse = coarse_inverse[0]
    corners = corner_map[0, 0]
    lengths = interface_tiles[0, 0] * TILE
    run_start = jnp.concatenate([jnp.zeros((1,), jnp.int32), jnp.cumsum(lengths)[:3]])
    dual_rows = operator.shape[0]
    live_mask = jnp.arange(dual_rows, dtype=jnp.int32)[:, None] < jnp.sum(lengths)
    onehot = (corners[:, None] == jnp.arange(NCOARSE, dtype=jnp.int32)[None, :]).astype(jnp.float32)

    def assemble(values_in):
        incoming = [None, None, None, None]
        for run_index, distance in enumerate((-2, -1, 1, 2)):
            outgoing = extract_run(values_in, run_start[3 - run_index], lengths[3 - run_index])
            incoming[run_index] = passed_along(outgoing, "sub", -distance)
        assembled = jnp.where(live_mask, values_in, jnp.zeros_like(values_in))
        for run_index in range(4):
            assembled = assembled + insert_run(incoming[run_index], run_start[run_index], dual_rows)
        return assembled

    residual = assemble(gap_terms[0, 0])
    direction = residual
    multipliers = jnp.zeros_like(residual)
    norm_now = lax.psum(jnp.sum(residual * residual, axis=0), ("cluster", "sub"))
    for iteration in range(ITERS):
        local_part = jnp.dot(
            operator, direction.astype(jnp.bfloat16), preferred_element_type=jnp.float32
        )
        corner_values = jnp.dot(coupling, direction, precision=highest)
        coarse_part = jnp.dot(onehot.T, corner_values, precision=highest)
        coarse_total = lax.psum(coarse_part, "cluster")
        coarse_solution = jnp.dot(inverse, coarse_total, precision=highest)
        corner_back = jnp.dot(onehot, coarse_solution, precision=highest)
        image = assemble(local_part + jnp.dot(coupling.T, corner_back, precision=highest))
        curvature = lax.psum(jnp.sum(direction * image, axis=0), ("cluster", "sub"))
        step_size = norm_now / curvature
        multipliers = multipliers + step_size * direction
        residual = residual - step_size * image
        norm_next = lax.psum(jnp.sum(residual * residual, axis=0), ("cluster", "sub"))
        direction = residual + norm_next / norm_now * direction
        norm_now = norm_next
    return (multipliers[None, None], residual[None, None])


def solution(mesh):
    in_specs = (
        P("cluster", "sub", None, None),
        P("cluster", "sub", None, None),
        P("sub", None, None),
        P("cluster", "sub", None),
        P("cluster", "sub", None),
        P("cluster", "sub", None, None),
    )
    out_specs = (P("cluster", "sub", None, None), P("cluster", "sub", None, None))
    return jax.shard_map(local, mesh=mesh, in_specs=in_specs, out_specs=out_specs, check_vma=False)
```

profile of v0, /device:TPU:1, one launch (start us, length us, event | category | flops | bytes accessed | tf_op | source)
XLA Modules:
  0.0 746.1 jit_solution(15423645180526299071)
XLA Ops:
  18.1 2.8 collective-permute-start.1
  22.6 4.8 collective-permute-start.3
  46.0 70.0 %all-reduce.9.cloned.1.call-done = f32[128,128]{1,0:T(8,128)} async-done(((f32[128,128]{1,0:T(8,128)}), f32[128,128]{1,0:T(8,128)}) %all-reduce.9.cloned.1.call-update) | async-done | bytes 65552 | tf_op jit(solution)/shard_map/psum | solution.py:62
  118.4 6.3 fusion.6
  125.8 6.7 collective-permute-start.5
  132.6 4.1 collective-permute-start.7
  147.2 2.8 multiply_reduce_fusion.4
  150.0 78.7 %all-reduce.4 = (f32[128]{0:T(128)S(1)}, f32[128]{0:T(128)S(1)}) all-reduce(f32[128]{0:T(128)} %get-tuple-element.5, f32[128]{0:T(128)} %get-tuple-element.4), channel_id=1, replica_groups=mesh['cluster'=8,'sub'=32] {'cluster','sub'}, use_global_device_ids=true, to_apply=%region_3.4 | all-reduce | flops 256 | bytes 2048 | tf_op jit(solution)/shard_map/psum | solution.py:55
  229.6 72.4 %psum.66 = f32[128]{0:T(128)S(1)} all-reduce(f32[128]{0:T(128)S(1)} %multiply_reduce_fusion.3), channel_id=1, replica_groups=mesh['cluster'=8,'sub'=32] {'cluster','sub'}, use_global_device_ids=true, to_apply=%region_8.9 | all-reduce | flops 128 | bytes 1024 | tf_op jit(solution)/shard_map/psum | solution.py:70
  305.5 7.2 fusion.2
  312.7 56.5 %all-reduce.11.cloned.1.call-done = f32[128,128]{1,0:T(8,128)} async-done(((f32[128,128]{1,0:T(8,128)}), f32[128,128]{1,0:T(8,128)}) %all-reduce.11.cloned.1.call-update) | async-done | bytes 65552 | tf_op jit(solution)/shard_map/psum | solution.py:62
  374.1 6.7 collective-permute-start.9
  381.5 3.6 collective-permute-start.11
  395.8 4.2 multiply_reduce_fusion.2
  400.0 78.7 %psum.68 = f32[128]{0:T(128)} all-reduce(f32[128]{0:T(128)} %get-tuple-element.12), channel_id=1, replica_groups=mesh['cluster'=8,'sub'=32] {'cluster','sub'}, use_global_device_ids=true, to_apply=%region_11.12 | all-reduce | flops 128 | bytes 1024 | tf_op jit(solution)/shard_map/psum | solution.py:66
  479.3 3.0 multiply_reduce_fusion.1
  482.3 72.5 %psum.69 = f32[128]{0:T(128)S(1)} all-reduce(f32[128]{0:T(128)} %get-tuple-element.10), channel_id=1, replica_groups=mesh['cluster'=8,'sub'=32] {'cluster','sub'}, use_global_device_ids=true, to_apply=%region_13.14 | all-reduce | flops 128 | bytes 1024 | tf_op jit(solution)/shard_map/psum | solution.py:70
  558.7 7.2 fusion
  565.9 56.7 %all-reduce.13.cloned.1.call-done = f32[128,128]{1,0:T(8,128)} async-done(((f32[128,128]{1,0:T(8,128)}), f32[128,128]{1,0:T(8,128)}) %all-reduce.13.cloned.1.call-update) | async-done | bytes 65552 | tf_op jit(solution)/shard_map/psum | solution.py:62
  627.4 6.7 collective-permute-start.13
  634.9 3.6 collective-permute-start.15
  649.1 3.7 multiply_reduce_fusion
  652.8 78.6 %psum.71 = f32[128]{0:T(128)} all-reduce(f32[128]{0:T(128)S(1)} %get-tuple-element.8), channel_id=1, replica_groups=mesh['cluster'=8,'sub'=32] {'cluster','sub'}, use_global_device_ids=true, to_apply=%region_16.17 | all-reduce | flops 128 | bytes 1024 | tf_op jit(solution)/shard_map/psum | solution.py:66
  732.1 3.3 subtract_bitcast_fusion
  (145 shorter events, 81.6 us)
Async XLA Ops:
  7.2 36.8 %copy-start = (f32[1,1,48,2048]{3,2,1,0:T(8,128)S(1)}, f32[1,1,48,2048]{3,2,1,0:T(8,128)}, u32[]{:S(2)}) copy-start(f32[1,1,48,2048]{3,2,1,0:T(8,128)} %param.7) | copy-start | bytes 1179652
  7.2 108.8 %all-reduce.9.cloned.1.call-start = ((), (), s32[]{:S(2)}) async-start(), calls=%async_computation | async-start | bytes 131072 | tf_op jit(solution)/shard_map/psum | solution.py:62
  18.1 14.6 %collective-permute-start.1 = (f32[512,128]{0,1:T(8,128)S(1)}, f32[512,128]{0,1:T(8,128)S(1)}, u32[]{:S(2)}, u32[]{:S(2)}) collective-permute-start(f32[512,128]{0,1:T(8,128)S(1)} %bitcast_select_fusion.2), channel_id=1, source_target_pairs={{31,0},{0,1},{1,2},{2,3},{3,4},{4,5},{5,6},{6,7},{7,8},{8,9},{9,10... | collective-permute-start | bytes 786440 | tf_op jit(solution)/shard_map/ppermute | solution.py:15
  21.0 14.7 %collective-permute-start.2 = (f32[512,128]{0,1:T(8,128)S(1)}, f32[512,128]{0,1:T(8,128)}, u32[]{:S(2)}, u32[]{:S(2)}) collective-permute-start(f32[512,128]{0,1:T(8,128)S(1)} %bitcast_select_fusion.1), channel_id=1, source_target_pairs={{1,0},{2,1},{3,2},{4,3},{5,4},{6,5},{7,6},{8,7},{9,8},{10,9},{11,1... | collective-permute-start | bytes 786440 | tf_op jit(solution)/shard_map/ppermute | solution.py:15
  22.6 9.4 %copy-start.7 = (pred[512]{0:T(512)(128)(4,1)}, pred[512]{0:T(512)(128)(4,1)S(1)}, u32[]{:S(2)}) copy-start(pred[512]{0:T(512)(128)(4,1)S(1)} %iota_compare_fusion.5) | copy-start | bytes 1540
  22.6 16.2 %collective-permute-start.3 = (f32[512,128]{0,1:T(8,128)S(1)}, f32[512,128]{0,1:T(8,128)S(1)}, u32[]{:S(2)}, u32[]{:S(2)}) collective-permute-start(f32[512,128]{0,1:T(8,128)S(1)} %fusion.38), channel_id=1, source_target_pairs={{2,0},{3,1},{4,2},{5,3},{6,4},{7,5},{8,6},{9,7},{10,8},{11,9},{12,... | collective-permute-start | bytes 786440 | tf_op jit(solution)/shard_map/ppermute | solution.py:15
  28.2 13.6 %collective-permute-start = (f32[512,128]{0,1:T(8,128)S(1)}, f32[512,128]{0,1:T(8,128)S(1)}, u32[]{:S(2)}, u32[]{:S(2)}) collective-permute-start(f32[512,128]{0,1:T(8,128)S(1)} %bitcast_select_fusion.3), channel_id=1, source_target_pairs={{30,0},{31,1},{0,2},{1,3},{2,4},{3,5},{4,6},{5,7},{6,8},{7,9},{8,1... | collective-permute-start | bytes 786440 | tf_op jit(solution)/shard_map/ppermute | solution.py:15
  44.0 72.0 %copy-start.5 = (f32[1,128,128]{2,1,0:T(8,128)S(1)}, f32[1,128,128]{2,1,0:T(8,128)}, u32[]{:S(2)}) copy-start(f32[1,128,128]{2,1,0:T(8,128)} %param.8) | copy-start | bytes 196612
  45.9 323.3 %all-reduce.11.cloned.1.call-start = ((), (), s32[]{:S(2)}) async-start(), calls=%async_computation.1 | async-start | bytes 131072 | tf_op jit(solution)/shard_map/psum | solution.py:62
  125.8 10.9 %collective-permute-start.5 = (f32[512,128]{0,1:T(8,128)S(1)}, f32[512,128]{0,1:T(8,128)S(1)}, u32[]{:S(2)}, u32[]{:S(2)}) collective-permute-start(f32[512,128]{0,1:T(8,128)S(1)} %get-tuple-element.23), channel_id=1, source_target_pairs={{31,0},{0,1},{1,2},{2,3},{3,4},{4,5},{5,6},{6,7},{7,8},{8,9},{9,10... | collective-permute-start | bytes 786440 | tf_op jit(solution)/shard_map/ppermute | solution.py:15
  132.5 8.6 %collective-permute-start.6 = (f32[512,128]{0,1:T(8,128)}, f32[512,128]{0,1:T(8,128)S(1)}, u32[]{:S(2)}, u32[]{:S(2)}) collective-permute-start(f32[512,128]{0,1:T(8,128)} %get-tuple-element.22), channel_id=1, source_target_pairs={{1,0},{2,1},{3,2},{4,3},{5,4},{6,5},{7,6},{8,7},{9,8},{10,9},{11,1... | collective-permute-start | bytes 786440 | tf_op jit(solution)/shard_map/ppermute | solution.py:15
  132.6 11.6 %collective-permute-start.7 = (f32[512,128]{0,1:T(8,128)S(1)}, f32[512,128]{0,1:T(8,128)S(1)}, u32[]{:S(2)}, u32[]{:S(2)}) collective-permute-start(f32[512,128]{0,1:T(8,128)S(1)} %slice_select_fusion.2), channel_id=1, source_target_pairs={{2,0},{3,1},{4,2},{5,3},{6,4},{7,5},{8,6},{9,7},{10,8},{11,9},{12,... | collective-permute-start | bytes 786440 | tf_op jit(solution)/shard_map/ppermute | solution.py:15
  136.7 10.5 %collective-permute-start.4 = (f32[512,128]{0,1:T(8,128)}, f32[512,128]{0,1:T(8,128)}, u32[]{:S(2)}, u32[]{:S(2)}) collective-permute-start(f32[512,128]{0,1:T(8,128)} %get-tuple-element.21), channel_id=1, source_target_pairs={{30,0},{31,1},{0,2},{1,3},{2,4},{3,5},{4,6},{5,7},{6,8},{7,9},{8,1... | collective-permute-start | bytes 786440 | tf_op jit(solution)/shard_map/ppermute | solution.py:15
  305.5 317.1 %all-reduce.13.cloned.1.call-start = ((), (), s32[]{:S(2)}) async-start(), calls=%async_computation.2 | async-start | bytes 131072 | tf_op jit(solution)/shard_map/psum | solution.py:62
  374.1 11.2 %collective-permute-start.9 = (f32[512,128]{0,1:T(8,128)S(1)}, f32[512,128]{0,1:T(8,128)}, u32[]{:S(2)}, u32[]{:S(2)}) collective-permute-start(f32[512,128]{0,1:T(8,128)S(1)} %get-tuple-element.20), channel_id=1, source_target_pairs={{31,0},{0,1},{1,2},{2,3},{3,4},{4,5},{5,6},{6,7},{7,8},{8,9},{9,10... | collective-permute-start | bytes 786440 | tf_op jit(solution)/shard_map/ppermute | solution.py:15
  380.8 8.8 %collective-permute-start.10 = (f32[512,128]{0,1:T(8,128)}, f32[512,128]{0,1:T(8,128)}, u32[]{:S(2)}, u32[]{:S(2)}) collective-permute-start(f32[512,128]{0,1:T(8,128)} %get-tuple-element.19), channel_id=1, source_target_pairs={{1,0},{2,1},{3,2},{4,3},{5,4},{6,5},{7,6},{8,7},{9,8},{10,9},{11,1... | collective-permute-start | bytes 786440 | tf_op jit(solution)/shard_map/ppermute | solution.py:15
  381.5 11.1 %collective-permute-start.11 = (f32[512,128]{0,1:T(8,128)}, f32[512,128]{0,1:T(8,128)}, u32[]{:S(2)}, u32[]{:S(2)}) collective-permute-start(f32[512,128]{0,1:T(8,128)} %slice_select_fusion.1), channel_id=1, source_target_pairs={{2,0},{3,1},{4,2},{5,3},{6,4},{7,5},{8,6},{9,7},{10,8},{11,9},{12,... | collective-permute-start | bytes 786440 | tf_op jit(solution)/shard_map/ppermute | solution.py:15
  385.1 10.7 %collective-permute-start.8 = (f32[512,128]{0,1:T(8,128)}, f32[512,128]{0,1:T(8,128)}, u32[]{:S(2)}, u32[]{:S(2)}) collective-permute-start(f32[512,128]{0,1:T(8,128)} %get-tuple-element.18), channel_id=1, source_target_pairs={{30,0},{31,1},{0,2},{1,3},{2,4},{3,5},{4,6},{5,7},{6,8},{7,9},{8,1... | collective-permute-start | bytes 786440 | tf_op jit(solution)/shard_map/ppermute | solution.py:15
  627.4 11.3 %collective-permute-start.13 = (f32[512,128]{0,1:T(8,128)S(1)}, f32[512,128]{0,1:T(8,128)}, u32[]{:S(2)}, u32[]{:S(2)}) collective-permute-start(f32[512,128]{0,1:T(8,128)S(1)} %get-tuple-element.17), channel_id=1, source_target_pairs={{31,0},{0,1},{1,2},{2,3},{3,4},{4,5},{5,6},{6,7},{7,8},{8,9},{9,10... | collective-permute-start | bytes 786440 | tf_op jit(solution)/shard_map/ppermute | solution.py:15
  634.1 8.7 %collective-permute-start.14 = (f32[512,128]{0,1:T(8,128)}, f32[512,128]{0,1:T(8,128)}, u32[]{:S(2)}, u32[]{:S(2)}) collective-permute-start(f32[512,128]{0,1:T(8,128)} %get-tuple-element.16), channel_id=1, source_target_pairs={{1,0},{2,1},{3,2},{4,3},{5,4},{6,5},{7,6},{8,7},{9,8},{10,9},{11,1... | collective-permute-start | bytes 786440 | tf_op jit(solution)/shard_map/ppermute | solution.py:15
  634.9 11.1 %collective-permute-start.15 = (f32[512,128]{0,1:T(8,128)}, f32[512,128]{0,1:T(8,128)}, u32[]{:S(2)}, u32[]{:S(2)}) collective-permute-start(f32[512,128]{0,1:T(8,128)} %slice_select_fusion), channel_id=1, source_target_pairs={{2,0},{3,1},{4,2},{5,3},{6,4},{7,5},{8,6},{9,7},{10,8},{11,9},{12,... | collective-permute-start | bytes 786440 | tf_op jit(solution)/shard_map/ppermute | solution.py:15
  638.5 10.7 %collective-permute-start.12 = (f32[512,128]{0,1:T(8,128)}, f32[512,128]{0,1:T(8,128)}, u32[]{:S(2)}, u32[]{:S(2)}) collective-permute-start(f32[512,128]{0,1:T(8,128)} %get-tuple-element.15), channel_id=1, source_target_pairs={{30,0},{31,1},{0,2},{1,3},{2,4},{3,5},{4,6},{5,7},{6,8},{7,9},{8,1... | collective-permute-start | bytes 786440 | tf_op jit(solution)/shard_map/ppermute | solution.py:15
  649.1 83.0 %copy-start.16 = (f32[128]{0:T(128)S(1)}, f32[128]{0:T(128)}, u32[]{:S(2)}) copy-start(f32[128]{0:T(128)} %copy-done.15) | copy-start | bytes 1540
  649.1 83.0 %copy-start.18 = (f32[128]{0:T(128)S(1)}, f32[128]{0:T(128)}, u32[]{:S(2)}) copy-start(f32[128]{0:T(128)} %copy-done.17) | copy-start | bytes 1540
  (16 other events, 73.1 us)
Sparse Core Ops, SparseCore 0:
  46.1 69.9 all-reduce.8
  305.6 63.6 all-reduce.10
  558.8 63.7 all-reduce.12
where the time goes:
time: 756 us; the launch traced here: 746 us
  blocking collectives  381 us (50%)
  waiting for transfers between devices  187 us (25%)
  local copies, waits for them, and re-layouts  45.1 us (6%)
  starting transfers between devices  40.2 us (5%)
  matrix products  36 us (5%)
  other arithmetic  33.2 us (4%)
  between operations  23.7 us (3%)
    psum x3, blocking collectives, local(): lax.psum(jnp.sum(residual * residual, axis=0), ('cluster', 'sub'))  224 us
    psum x3, waiting for transfers between devices, local(): coarse_total = lax.psum(coarse_part, 'cluster')  183 us
    psum x2, blocking collectives, local(): curvature = lax.psum(jnp.sum(direction * image, axis=0), ('cluster', 'sub'))  157 us
    ppermute x16, starting transfers between devices, passed_along(): return lax.ppermute(block, axis, route)  40 us
    dynamic_update_slice x12, local copies, waits for them, and re-layouts, insert_run(): lax.dynamic_update_slice_in_dim(padded, run_block, start_row, 0)[:dual_rows]  22.4 us
    dot_general x3, matrix products, local(): jnp.dot(operator, direction.astype(jnp.bfloat16), preferred_element_type=...  20.7 us
  transfers between devices with their start and end apart: 19, of which 6 were waited for; matrix products, arithmetic and copies ran while one was open for 7% of the time, Pallas kernels for 0%

commit v1 on v0

--- a/solution.py
+++ b/solution.py
@@ -63,7 +63,9 @@
         coarse_solution = jnp.dot(inverse, coarse_total, precision=highest)
         corner_back = jnp.dot(onehot, coarse_solution, precision=highest)
         image = assemble(local_part + jnp.dot(coupling.T, corner_back, precision=highest))
-        curvature = lax.psum(jnp.sum(direction * image, axis=0), ("cluster", "sub"))
+        chunk = jnp.sum(direction * image, axis=0)
+        small = lax.all_gather(chunk, ("cluster", "sub"))
+        curvature = jnp.sum(small, 0)
         step_size = norm_now / curvature
         multipliers = multipliers + step_size * direction
         residual = residual - step_size * image

time: 756 us -> 779 us (1.030)
  blocking collectives: 381 us -> 402 us
    all_gather x0 -> x3, blocking collectives: none -> 181 us  [local(): small = lax.all_gather(chunk, ('cluster', 'sub'))]
    psum x2 -> x0, blocking collectives: 157 us -> none  [local(): curvature = lax.psum(jnp.sum(direction * image, axis=0), ('cluster', 'sub'))]
where the time goes in v1:
time: 779 us; the launch traced here: 770 us
  blocking collectives  402 us (52%)
  waiting for transfers between devices  186 us (24%)
  local copies, waits for them, and re-layouts  45.2 us (6%)
  starting transfers between devices  40.2 us (5%)
  matrix products  36 us (5%)
  other arithmetic  35.9 us (5%)
  between operations  24.2 us (3%)
    psum x3, blocking collectives, local(): lax.psum(jnp.sum(residual * residual, axis=0), ('cluster', 'sub'))  222 us
    psum x3, waiting for transfers between devices, local(): coarse_total = lax.psum(coarse_part, 'cluster')  182 us
    all_gather x3, blocking collectives, local(): small = lax.all_gather(chunk, ('cluster', 'sub'))  181 us
    ppermute x16, starting transfers between devices, passed_along(): return lax.ppermute(block, axis, route)  40 us
    dynamic_update_slice x12, local copies, waits for them, and re-layouts, insert_run(): lax.dynamic_update_slice_in_dim(padded, run_block, start_row, 0)[:dual_rows]  22.4 us
    dot_general x3, matrix products, local(): jnp.dot(operator, direction.astype(jnp.bfloat16), preferred_element_type=...  20.7 us
  transfers between devices with their start and end apart: 19, of which 6 were waited for; matrix products, arithmetic and copies ran while one was open for 7% of the time, Pallas kernels for 0%

profile of v1, /device:TPU:1, one launch (start us, length us, event | category | flops | bytes accessed | tf_op | source)
XLA Modules:
  0.0 769.5 jit_solution(7975096518692466637)
XLA Ops:
  23.0 4.8 collective-permute-start.3
  46.6 70.0 %all-reduce.8.cloned.1.call-done = f32[128,128]{1,0:T(8,128)} async-done(((f32[128,128]{1,0:T(8,128)}), f32[128,128]{1,0:T(8,128)}) %all-reduce.8.cloned.1.call-update) | async-done | bytes 65552 | tf_op jit(solution)/shard_map/psum | solution.py:62
  119.1 6.3 fusion.6
  126.4 6.7 collective-permute-start.5
  133.2 4.1 collective-permute-start.7
  147.8 2.8 multiply_reduce_fusion.4
  150.6 57.8 %all-gather.3 = f32[256,1,128]{2,1,0:T(1,128)S(1)} all-gather(f32[1,1,128]{2,1,0:T(1,128)S(1)} %bitcast.111), channel_id=2, replica_groups=mesh['cluster'=8,'sub'=32] {'cluster','sub'}, dimensions={0}, use_global_device_ids=true | all-gather | bytes 131584 | tf_op jit(solution)/shard_map/all_gather | solution.py:67
  208.4 73.7 %psum.42 = f32[128]{0:T(128)S(1)} all-reduce(f32[128]{0:T(128)} %get-tuple-element.7), channel_id=1, replica_groups=mesh['cluster'=8,'sub'=32] {'cluster','sub'}, use_global_device_ids=true, to_apply=%region_3.4 | all-reduce | flops 128 | bytes 1024 | tf_op jit(solution)/shard_map/psum | solution.py:55
  283.3 73.6 %psum.44 = f32[128]{0:T(128)S(1)} all-reduce(f32[128]{0:T(128)S(1)} %multiply_reduce_fusion.3), channel_id=1, replica_groups=mesh['cluster'=8,'sub'=32] {'cluster','sub'}, use_global_device_ids=true, to_apply=%region_8.9 | all-reduce | flops 128 | bytes 1024 | tf_op jit(solution)/shard_map/psum | solution.py:72
  360.4 7.2 fusion.2
  367.6 55.9 %all-reduce.10.cloned.1.call-done = f32[128,128]{1,0:T(8,128)} async-done(((f32[128,128]{1,0:T(8,128)}), f32[128,128]{1,0:T(8,128)}) %all-reduce.10.cloned.1.call-update) | async-done | bytes 65552 | tf_op jit(solution)/shard_map/psum | solution.py:62
  428.3 6.7 collective-permute-start.9
  435.8 3.6 collective-permute-start.11
  450.0 3.7 multiply_reduce_fusion.2
  453.7 61.4 %all-gather.4 = f32[256,1,128]{2,1,0:T(1,128)} all-gather(f32[1,1,128]{2,1,0:T(1,128)S(1)} %bitcast.113), channel_id=3, replica_groups=mesh['cluster'=8,'sub'=32] {'cluster','sub'}, dimensions={0}, use_global_device_ids=true | all-gather | bytes 131584 | tf_op jit(solution)/shard_map/all_gather | solution.py:67
  517.4 3.0 multiply_reduce_fusion.1
  520.4 74.5 %psum.46 = f32[128]{0:T(128)S(1)} all-reduce(f32[128]{0:T(128)} %get-tuple-element.10), channel_id=1, replica_groups=mesh['cluster'=8,'sub'=32] {'cluster','sub'}, use_global_device_ids=true, to_apply=%region_13.14 | all-reduce | flops 128 | bytes 1024 | tf_op jit(solution)/shard_map/psum | solution.py:72
  598.8 7.2 fusion
  606.1 56.0 %all-reduce.12.cloned.1.call-done = f32[128,128]{1,0:T(8,128)} async-done(((f32[128,128]{1,0:T(8,128)}), f32[128,128]{1,0:T(8,128)}) %all-reduce.12.cloned.1.call-update) | async-done | bytes 65552 | tf_op jit(solution)/shard_map/psum | solution.py:62
  666.9 6.7 collective-permute-start.13
  674.4 3.6 collective-permute-start.15
  688.6 3.7 multiply_reduce_fusion
  692.3 61.4 %all-gather.5 = f32[256,1,128]{2,1,0:T(1,128)} all-gather(f32[1,1,128]{2,1,0:T(1,128)S(1)} %bitcast.112), channel_id=4, replica_groups=mesh['cluster'=8,'sub'=32] {'cluster','sub'}, dimensions={0}, use_global_device_ids=true | all-gather | bytes 131584 | tf_op jit(solution)/shard_map/all_gather | solution.py:67
  755.5 3.3 subtract_bitcast_fusion
  (149 shorter events, 87.7 us)
Async XLA Ops:
  7.2 37.4 %copy-start = (f32[1,1,48,2048]{3,2,1,0:T(8,128)S(1)}, f32[1,1,48,2048]{3,2,1,0:T(8,128)}, u32[]{:S(2)}) copy-start(f32[1,1,48,2048]{3,2,1,0:T(8,128)} %param.7) | copy-start | bytes 1179652
  7.2 109.5 %all-reduce.8.cloned.1.call-start = ((), (), s32[]{:S(2)}) async-start(), calls=%async_computation | async-start | bytes 131072 | tf_op jit(solution)/shard_map/psum | solution.py:62
  18.4 14.8 %collective-permute-start.1 = (f32[512,128]{0,1:T(8,128)S(1)}, f32[512,128]{0,1:T(8,128)S(1)}, u32[]{:S(2)}, u32[]{:S(2)}) collective-permute-start(f32[512,128]{0,1:T(8,128)S(1)} %bitcast_select_fusion.2), channel_id=1, source_target_pairs={{31,0},{0,1},{1,2},{2,3},{3,4},{4,5},{5,6},{6,7},{7,8},{8,9},{9,10... | collective-permute-start | bytes 786440 | tf_op jit(solution)/shard_map/ppermute | solution.py:15
  21.4 14.9 %collective-permute-start.2 = (f32[512,128]{0,1:T(8,128)S(1)}, f32[512,128]{0,1:T(8,128)}, u32[]{:S(2)}, u32[]{:S(2)}) collective-permute-start(f32[512,128]{0,1:T(8,128)S(1)} %bitcast_select_fusion.1), channel_id=1, source_target_pairs={{1,0},{2,1},{3,2},{4,3},{5,4},{6,5},{7,6},{8,7},{9,8},{10,9},{11,1... | collective-permute-start | bytes 786440 | tf_op jit(solution)/shard_map/ppermute | solution.py:15
  22.9 9.6 %copy-start.7 = (pred[512]{0:T(512)(128)(4,1)}, pred[512]{0:T(512)(128)(4,1)S(1)}, u32[]{:S(2)}) copy-start(pred[512]{0:T(512)(128)(4,1)S(1)} %iota_compare_fusion.5) | copy-start | bytes 1540
  23.0 16.4 %collective-permute-start.3 = (f32[512,128]{0,1:T(8,128)S(1)}, f32[512,128]{0,1:T(8,128)S(1)}, u32[]{:S(2)}, u32[]{:S(2)}) collective-permute-start(f32[512,128]{0,1:T(8,128)S(1)} %fusion.38), channel_id=1, source_target_pairs={{2,0},{3,1},{4,2},{5,3},{6,4},{7,5},{8,6},{9,7},{10,8},{11,9},{12,... | collective-permute-start | bytes 786440 | tf_op jit(solution)/shard_map/ppermute | solution.py:15
  28.6 13.8 %collective-permute-start = (f32[512,128]{0,1:T(8,128)S(1)}, f32[512,128]{0,1:T(8,128)S(1)}, u32[]{:S(2)}, u32[]{:S(2)}) collective-permute-start(f32[512,128]{0,1:T(8,128)S(1)} %bitcast_select_fusion.3), channel_id=1, source_target_pairs={{30,0},{31,1},{0,2},{1,3},{2,4},{3,5},{4,6},{5,7},{6,8},{7,9},{8,1... | collective-permute-start | bytes 786440 | tf_op jit(solution)/shard_map/ppermute | solution.py:15
  44.6 72.0 %copy-start.5 = (f32[1,128,128]{2,1,0:T(8,128)S(1)}, f32[1,128,128]{2,1,0:T(8,128)}, u32[]{:S(2)}) copy-start(f32[1,128,128]{2,1,0:T(8,128)} %param.8) | copy-start | bytes 196612
  46.6 376.9 %all-reduce.10.cloned.1.call-start = ((), (), s32[]{:S(2)}) async-start(), calls=%async_computation.1 | async-start | bytes 131072 | tf_op jit(solution)/shard_map/psum | solution.py:62
  126.4 10.9 %collective-permute-start.5 = (f32[512,128]{0,1:T(8,128)S(1)}, f32[512,128]{0,1:T(8,128)S(1)}, u32[]{:S(2)}, u32[]{:S(2)}) collective-permute-start(f32[512,128]{0,1:T(8,128)S(1)} %get-tuple-element.23), channel_id=1, source_target_pairs={{31,0},{0,1},{1,2},{2,3},{3,4},{4,5},{5,6},{6,7},{7,8},{8,9},{9,10... | collective-permute-start | bytes 786440 | tf_op jit(solution)/shard_map/ppermute | solution.py:15
  133.1 8.6 %collective-permute-start.6 = (f32[512,128]{0,1:T(8,128)}, f32[512,128]{0,1:T(8,128)S(1)}, u32[]{:S(2)}, u32[]{:S(2)}) collective-permute-start(f32[512,128]{0,1:T(8,128)} %get-tuple-element.22), channel_id=1, source_target_pairs={{1,0},{2,1},{3,2},{4,3},{5,4},{6,5},{7,6},{8,7},{9,8},{10,9},{11,1... | collective-permute-start | bytes 786440 | tf_op jit(solution)/shard_map/ppermute | solution.py:15
  133.2 11.6 %collective-permute-start.7 = (f32[512,128]{0,1:T(8,128)S(1)}, f32[512,128]{0,1:T(8,128)S(1)}, u32[]{:S(2)}, u32[]{:S(2)}) collective-permute-start(f32[512,128]{0,1:T(8,128)S(1)} %slice_select_fusion.2), channel_id=1, source_target_pairs={{2,0},{3,1},{4,2},{5,3},{6,4},{7,5},{8,6},{9,7},{10,8},{11,9},{12,... | collective-permute-start | bytes 786440 | tf_op jit(solution)/shard_map/ppermute | solution.py:15
  137.3 10.5 %collective-permute-start.4 = (f32[512,128]{0,1:T(8,128)}, f32[512,128]{0,1:T(8,128)}, u32[]{:S(2)}, u32[]{:S(2)}) collective-permute-start(f32[512,128]{0,1:T(8,128)} %get-tuple-element.21), channel_id=1, source_target_pairs={{30,0},{31,1},{0,2},{1,3},{2,4},{3,5},{4,6},{5,7},{6,8},{7,9},{8,1... | collective-permute-start | bytes 786440 | tf_op jit(solution)/shard_map/ppermute | solution.py:15
  360.3 301.8 %all-reduce.12.cloned.1.call-start = ((), (), s32[]{:S(2)}) async-start(), calls=%async_computation.2 | async-start | bytes 131072 | tf_op jit(solution)/shard_map/psum | solution.py:62
  428.3 11.2 %collective-permute-start.9 = (f32[512,128]{0,1:T(8,128)S(1)}, f32[512,128]{0,1:T(8,128)}, u32[]{:S(2)}, u32[]{:S(2)}) collective-permute-start(f32[512,128]{0,1:T(8,128)S(1)} %get-tuple-element.20), channel_id=1, source_target_pairs={{31,0},{0,1},{1,2},{2,3},{3,4},{4,5},{5,6},{6,7},{7,8},{8,9},{9,10... | collective-permute-start | bytes 786440 | tf_op jit(solution)/shard_map/ppermute | solution.py:15
  435.0 8.8 %collective-permute-start.10 = (f32[512,128]{0,1:T(8,128)}, f32[512,128]{0,1:T(8,128)}, u32[]{:S(2)}, u32[]{:S(2)}) collective-permute-start(f32[512,128]{0,1:T(8,128)} %get-tuple-element.19), channel_id=1, source_target_pairs={{1,0},{2,1},{3,2},{4,3},{5,4},{6,5},{7,6},{8,7},{9,8},{10,9},{11,1... | collective-permute-start | bytes 786440 | tf_op jit(solution)/shard_map/ppermute | solution.py:15
  435.8 11.1 %collective-permute-start.11 = (f32[512,128]{0,1:T(8,128)}, f32[512,128]{0,1:T(8,128)}, u32[]{:S(2)}, u32[]{:S(2)}) collective-permute-start(f32[512,128]{0,1:T(8,128)} %slice_select_fusion.1), channel_id=1, source_target_pairs={{2,0},{3,1},{4,2},{5,3},{6,4},{7,5},{8,6},{9,7},{10,8},{11,9},{12,... | collective-permute-start | bytes 786440 | tf_op jit(solution)/shard_map/ppermute | solution.py:15
  439.3 10.6 %collective-permute-start.8 = (f32[512,128]{0,1:T(8,128)}, f32[512,128]{0,1:T(8,128)}, u32[]{:S(2)}, u32[]{:S(2)}) collective-permute-start(f32[512,128]{0,1:T(8,128)} %get-tuple-element.18), channel_id=1, source_target_pairs={{30,0},{31,1},{0,2},{1,3},{2,4},{3,5},{4,6},{5,7},{6,8},{7,9},{8,1... | collective-permute-start | bytes 786440 | tf_op jit(solution)/shard_map/ppermute | solution.py:15
  666.9 11.3 %collective-permute-start.13 = (f32[512,128]{0,1:T(8,128)S(1)}, f32[512,128]{0,1:T(8,128)}, u32[]{:S(2)}, u32[]{:S(2)}) collective-permute-start(f32[512,128]{0,1:T(8,128)S(1)} %get-tuple-element.17), channel_id=1, source_target_pairs={{31,0},{0,1},{1,2},{2,3},{3,4},{4,5},{5,6},{6,7},{7,8},{8,9},{9,10... | collective-permute-start | bytes 786440 | tf_op jit(solution)/shard_map/ppermute | solution.py:15
  673.6 8.8 %collective-permute-start.14 = (f32[512,128]{0,1:T(8,128)}, f32[512,128]{0,1:T(8,128)}, u32[]{:S(2)}, u32[]{:S(2)}) collective-permute-start(f32[512,128]{0,1:T(8,128)} %get-tuple-element.16), channel_id=1, source_target_pairs={{1,0},{2,1},{3,2},{4,3},{5,4},{6,5},{7,6},{8,7},{9,8},{10,9},{11,1... | collective-permute-start | bytes 786440 | tf_op jit(solution)/shard_map/ppermute | solution.py:15
  674.4 11.2 %collective-permute-start.15 = (f32[512,128]{0,1:T(8,128)}, f32[512,128]{0,1:T(8,128)}, u32[]{:S(2)}, u32[]{:S(2)}) collective-permute-start(f32[512,128]{0,1:T(8,128)} %slice_select_fusion), channel_id=1, source_target_pairs={{2,0},{3,1},{4,2},{5,3},{6,4},{7,5},{8,6},{9,7},{10,8},{11,9},{12,... | collective-permute-start | bytes 786440 | tf_op jit(solution)/shard_map/ppermute | solution.py:15
  677.9 10.7 %collective-permute-start.12 = (f32[512,128]{0,1:T(8,128)}, f32[512,128]{0,1:T(8,128)}, u32[]{:S(2)}, u32[]{:S(2)}) collective-permute-start(f32[512,128]{0,1:T(8,128)} %get-tuple-element.15), channel_id=1, source_target_pairs={{30,0},{31,1},{0,2},{1,3},{2,4},{3,5},{4,6},{5,7},{6,8},{7,9},{8,1... | collective-permute-start | bytes 786440 | tf_op jit(solution)/shard_map/ppermute | solution.py:15
  688.6 66.9 %copy-start.16 = (f32[128]{0:T(128)S(1)}, f32[128]{0:T(128)}, u32[]{:S(2)}) copy-start(f32[128]{0:T(128)} %copy-done.15) | copy-start | bytes 1540
  688.6 66.9 %copy-start.18 = (f32[128]{0:T(128)S(1)}, f32[128]{0:T(128)}, u32[]{:S(2)}) copy-start(f32[128]{0:T(128)} %copy-done.17) | copy-start | bytes 1540
  (16 other events, 73.4 us)
Sparse Core Ops, SparseCore 0:
  46.7 69.9 all-reduce.7
  360.4 63.0 all-reduce.9
  599.0 63.0 all-reduce.11
